TPU v7x, 256 devices: a whole 4x4x8 slice. The times are simulated.
256 devices in a mesh: shard: 64 (over z, y_hi, x), tensor: 4 (over y_lo, core).
Axes of the slice: x: 4, y: 4 (y_hi: 2, y_lo: 2; y = y_hi * 2 + y_lo), z: 8, core: 2. Of those that a mesh axis runs over, the one named last changes fastest.
Arguments:
- acts: bfloat16 [131072, 2048], P('shard', 'tensor'), may hold values from -6 to 6
- out_grad: bfloat16 [131072, 1920], P('shard'), may hold values from -6 to 6
- sample_rows: int32 [4096], P('shard'), may hold values from 0 to 2047
- own_a: int32 [4, 4], replicated, may hold values from 0 to 3, each once within a row
- own_g: int32 [4, 5], replicated, may hold values from 0 to 4, each once within a row
- a_state: float32 [4, 4, 128, 128], P('tensor'), as said below
- g_state: float32 [4, 5, 96, 96], P('tensor'), as said below
- momentum: float32 [1920, 2048], P('shard', 'tensor'), may hold values from -6 to 6
- weight: float32 [1920, 2048], P('shard', 'tensor'), may hold values from -6 to 6
Outputs:
- a_state_new: float32 [4, 4, 128, 128], P('tensor')
- g_state_new: float32 [4, 5, 96, 96], P('tensor')
- momentum_new: float32 [1920, 2048], P('shard', 'tensor')
- weight_new: float32 [1920, 2048], P('shard', 'tensor')
- weight_bf16: bfloat16 [1920, 2048], P(None, 'tensor')
Inputs may be any that keep to these rules, and one draw needn't show every extreme that they name: `own_a`: slot s of a group is owned by the shard index s times the whole part of the shard axis's size over the group's number of slots. `own_g`: slot s of a group is owned by the shard index s times the whole part of the shard axis's size over the group's number of slots. `a_state`: every slot is symmetric positive definite. `g_state`: every slot is symmetric positive definite.
All inputs are finite; a program needn't handle non-finite values. Where the computation divides by a largest or mean magnitude, that divisor is 1e-20 or more.
Results may differ from a plain program's by a relative error of at most 0.0004.
Values may be sent and summed in bfloat16 or wider, within the bound.
A program may use at most 64 MiB of HBM per device.

v0:
```python
import jax
import jax.numpy as jnp
from jax import lax
from jax.sharding import PartitionSpec as P

NS_IT = 5


factor_decay = 0.8
damping_rate = 0.03
momentum_rate = 0.9
decay_rate = 0.01
learn_rate = 0.05
epsilon_sq = 1e-06
highest = lax.Precision.HIGHEST


def newton_inverse(factor):
    width = factor.shape[-1]
    identity = jnp.eye(width, dtype=jnp.float32)
    trace_mean = jnp.trace(factor, axis1=-2, axis2=-1) / width
    damped = factor + damping_rate * trace_mean[:, None, None] * identity
    bound = jnp.max(jnp.sum(jnp.abs(damped), axis=-1), axis=-1)
    guess = identity[None] / bound[:, None, None]
    for iteration in range(NS_IT):
        product = jnp.einsum("bij,bjk->bik", damped, guess, precision=highest)
        guess = jnp.einsum("bij,bjk->bik", guess, 2.0 * identity - product, precision=highest)
    return guess


def local_stats(rows, width):
    blocks = rows.reshape(rows.shape[0], -1, width)
    return jnp.einsum("sbi,sbj->bij", blocks, blocks, preferred_element_type=jnp.float32)


def owner_part(slots, shard_pos, shard_count):
    count = slots.shape[0]
    stride = shard_count // count
    slot_pos = jnp.minimum(shard_pos // stride, count - 1)
    mine = lax.dynamic_index_in_dim(slots, slot_pos, 0, keepdims=True)
    inverse = newton_inverse(mine)
    marker = (jnp.arange(count, dtype=jnp.int32) * stride == shard_pos).astype(jnp.float32)
    return marker[:, None, None] * inverse


def local(acts, out_grad, sample_rows, own_a, own_g, a_state, g_state, momentum, weight):
    shard_count = lax.axis_size("shard")
    tensor_count = lax.axis_size("tensor")
    shard_pos = lax.axis_index("shard")
    tensor_pos = lax.axis_index("tensor")
    block_a = a_state.shape[-1]
    block_g = g_state.shape[-1]
    samples = sample_rows.shape[0] * shard_count
    fresh_share = (1.0 - factor_decay) / samples
    picked_a = jnp.take(acts, sample_rows, axis=0)
    picked_g = jnp.take(out_grad, sample_rows, axis=0)
    group_cols = out_grad.shape[1] // tensor_count
    picked_g = lax.dynamic_slice_in_dim(picked_g, tensor_pos * group_cols, group_cols, 1)
    stats_a = local_stats(picked_a, block_a)
    stats_g = local_stats(picked_g, block_g)
    row_a = lax.dynamic_index_in_dim(own_a, tensor_pos, 0, keepdims=False)
    row_g = lax.dynamic_index_in_dim(own_g, tensor_pos, 0, keepdims=False)
    select_a = (row_a[None, :] == jnp.arange(row_a.shape[0], dtype=jnp.int32)[:, None]).astype(
        jnp.float32
    )
    select_g = (row_g[None, :] == jnp.arange(row_g.shape[0], dtype=jnp.int32)[:, None]).astype(
        jnp.float32
    )
    summed_a, summed_g = lax.psum((fresh_share * stats_a, fresh_share * stats_g), "shard")
    stored_a = jnp.einsum("sb,sij->bij", select_a, a_state[0], precision=highest)
    stored_g = jnp.einsum("sb,sij->bij", select_g, g_state[0], precision=highest)
    fac_a = factor_decay * stored_a + summed_a
    fac_g = factor_decay * stored_g + summed_g
    slots_a = jnp.einsum("sb,bij->sij", select_a, fac_a, precision=highest)
    slots_g = jnp.einsum("sb,bij->sij", select_g, fac_g, precision=highest)
    new_a_state = slots_a[None]
    new_g_state = slots_g[None]
    slot_inv_a, slot_inv_g = lax.psum(
        (owner_part(slots_a, shard_pos, shard_count), owner_part(slots_g, shard_pos, shard_count)),
        "shard",
    )
    inv_a = jnp.einsum("sb,sij->bij", select_a, slot_inv_a, precision=highest)
    local_inv_g = jnp.einsum("sb,sij->bij", select_g, slot_inv_g, precision=highest)
    inv_g = lax.all_gather(local_inv_g, "tensor", axis=0, tiled=True)
    raw_product = lax.dot_general(
        out_grad, acts, (((0,), (0,)), ((), ())), preferred_element_type=jnp.float32
    )
    left_done = jnp.einsum(
        "bij,bjd->bid", inv_g, raw_product.reshape(inv_g.shape[0], block_g, -1), precision=highest
    ).reshape(raw_product.shape)
    owned_rows = lax.psum_scatter(left_done, "shard", scatter_dimension=0, tiled=True)
    precon = jnp.einsum(
        "qbi,bij->qbj",
        owned_rows.reshape(owned_rows.shape[0], -1, block_a),
        inv_a,
        precision=highest,
    ).reshape(owned_rows.shape)
    square_total = lax.psum(jnp.sum(precon * precon), ("shard", "tensor"))
    mean_sq = square_total / (momentum.shape[0] * shard_count * momentum.shape[1] * tensor_count)
    update = precon / jnp.sqrt(mean_sq + epsilon_sq)
    momentum_new = momentum_rate * momentum + update + decay_rate * weight
    weight_new = weight - learn_rate * momentum_new
    gathered = lax.all_gather(weight_new.astype(jnp.bfloat16), "shard", axis=0, tiled=True)
    return (new_a_state, new_g_state, momentum_new, weight_new, gathered)


def solution(mesh):
    return jax.shard_map(
        local,
        mesh=mesh,
        in_specs=(
            P("shard", "tensor"),
            P("shard", None),
            P("shard"),
            P(),
            P(),
            P("tensor", None, None, None),
            P("tensor", None, None, None),
            P("shard", "tensor"),
            P("shard", "tensor"),
        ),
        out_specs=(
            P("tensor", None, None, None),
            P("tensor", None, None, None),
            P("shard", "tensor"),
            P("shard", "tensor"),
            P(None, "tensor"),
        ),
        check_vma=False,
    )
```

profile of v0, /device:TPU:24, one launch (start us, length us, event | category | flops | bytes accessed | tf_op | source)
XLA Modules:
  0.0 1844.4 jit_solution(15552979911411866139)
XLA Ops:
  7.2 0.8 compare_and_fusion
  8.1 0.7 compare_select_fusion
  8.8 0.7 gather_fusion
  9.5 5.2 gather_fusion.1
  14.7 1.0 convolution_multiply_fusion
  16.0 0.9 convolution_multiply_fusion.1
  17.0 0.7 fusion.41
  17.7 0.7 fusion.42
  18.4 0.5 fusion.10
  18.9 0.5 fusion.3
  19.4 692.7 %all-reduce.9.cloned.1.call-done = (f32[4,128,128]{2,1,0:T(8,128)}, f32[5,96,96]{2,1,0:T(8,128)}) async-done(((f32[4,128,128]{2,1,0:T(8,128)}, f32[5,96,96]{2,1,0:T(8,128)}), (f32[4,128,128]{2,1,0:T(8,128)}, f32[5,96,96]{2,1,0:T(8,128)})) %all-reduce.9.cloned.1.call-update) | async-done | bytes 446480 | tf_op jit(solution)/shard_map/psum | solution.py:69
  712.1 1.0 fusion.9
  713.1 0.6 fusion.7
  713.7 1.0 fusion.12
  714.7 0.5 fusion.1
  715.3 0.7 select_reduce_fusion
  716.7 1.0 abs_reduce_fusion
  717.7 0.6 reduce_max.18
  719.0 0.2 convolution_subtract_fusion.4
  719.2 0.2 fusion.13
  719.4 0.2 convolution_subtract_fusion.3
  719.7 0.2 fusion.52
  719.9 0.2 convolution_subtract_fusion.2
  720.1 0.2 fusion.53
  720.3 0.2 convolution_subtract_fusion.1
  720.5 0.2 fusion.54
  720.7 0.2 convolution_subtract_fusion
  720.9 0.2 fusion.55
  721.1 0.7 select_reduce_fusion.1
  722.5 0.8 abs_reduce_fusion.1
  723.3 0.6 reduce_max.19
  724.6 0.2 convolution_subtract_fusion.9
  724.8 0.2 fusion.20
  725.4 0.2 convolution_subtract_fusion.7
  725.5 0.2 fusion.57
  725.7 0.2 convolution_subtract_fusion.6
  725.9 0.2 fusion.58
  726.1 0.2 convolution_subtract_fusion.5
  726.3 0.2 fusion.59
  726.5 0.8 broadcast_multiply_fusion.1
  727.3 0.8 broadcast_multiply_fusion
  728.2 0.2 all-gather.3.cloned.1.call-start
  728.4 9.4 fusion.60
  737.8 0.6 dynamic-slice.4
  739.0 651.6 %all-reduce.7.cloned.1.call-done = (f32[4,128,128]{2,0,1:T(4,128)}, f32[5,96,96]{2,0,1:T(8,128)}) async-done(((f32[4,128,128]{2,0,1:T(4,128)}, f32[5,96,96]{2,0,1:T(8,128)}), (f32[4,128,128]{2,0,1:T(4,128)}, f32[5,96,96]{2,0,1:T(8,128)})) %all-reduce.7.cloned.1.call-update) | async-done | bytes 446480 | tf_op jit(solution)/shard_map/psum | solution.py:78
  1390.7 1.4 fusion.33
  1392.1 9.0 all_gather.6
  1401.1 7.5 fusion.61
  1408.6 198.0 %fusion = f32[32,512]{1,0:T(8,128)S(1)} fusion(f32[1920,512]{1,0:T(8,128)} %bitcast.83), kind=kCustom, calls=%all-reduce-scatter | all-reduce-scatter fusion | flops 1048577 | bytes 3998720
  1606.6 1.9 collective-permute-start.2
  1608.6 1.9 collective-permute-start.1
  1610.5 1.9 collective-permute-start
  1612.4 1.9 collective-permute-start.3
  1614.3 0.4 fusion.48
  1614.8 11.8 collective-permute-done.3
  1626.6 0.6 copy-done.4
  1627.2 2.1 concatenate
  1629.4 0.9 multiply_reduce_fusion
  1630.4 88.1 %psum.39 = f32[]{:T(128)} all-reduce(f32[]{:T(128)} %get-tuple-element.36), channel_id=1, replica_groups=mesh['shard'=64,'tensor'=4] {'shard','tensor'}, use_global_device_ids=true, to_apply=%region_12.13 | all-reduce | flops 1 | bytes 8 | tf_op jit(solution)/shard_map/psum | solution.py:98
  1719.2 1.6 convert_bitcast_fusion
  1720.8 0.7 copy.50
  1721.5 0.7 copy.51
  1722.3 111.8 %all-gather.3.cloned.1.call-done = bf16[64,30,512]{2,1,0:T(8,128)(2,1)} async-done(((bf16[1,30,512]{2,1,0:T(8,128)(2,1)}), bf16[64,30,512]{2,1,0:T(8,128)(2,1)}) %all-gather.3.cloned.1.call-update) | async-done | bytes 1966096 | tf_op jit(solution)/shard_map/all_gather | solution.py:103
  1834.1 3.8 reshape.250
  (34 shorter events, 1.0 us)
Async XLA Ops:
  7.2 1.6 copy-start
  7.2 11.2 copy-start.2
  7.2 11.7 copy-start.1
  7.2 704.9 %all-reduce.9.cloned.1.call-start = ((), (), s32[]{:S(2)}) async-start(), calls=%async_computation.2 | async-start | bytes 1015808 | tf_op jit(solution)/shard_map/psum | solution.py:69
  16.9 1373.8 %all-reduce.7.cloned.1.call-start = ((), (), s32[]{:S(2)}) async-start(), calls=%async_computation.1 | async-start | bytes 1310720 | tf_op jit(solution)/shard_map/psum | solution.py:78
  728.2 9.6 copy-start.5
  728.2 1105.9 %all-gather.3.cloned.1.call-start = ((), (), s32[]{:S(2)}) async-start(), calls=%async_computation | async-start | bytes 2129920 | tf_op jit(solution)/shard_map/all_gather | solution.py:103
  1408.6 205.7 %copy-start.3 = (f32[4,128,128]{2,0,1:T(4,128)S(1)}, f32[4,128,128]{2,0,1:T(4,128)}, u32[]{:S(2)}) copy-start(f32[4,128,128]{2,0,1:T(4,128)} %get-tuple-element.25) | copy-start | bytes 786436
  1606.6 19.9 %collective-permute-start.2 = (f32[32,512]{1,0:T(8,128)S(1)}, f32[32,512]{1,0:T(8,128)S(1)}, u32[]{:S(2)}, u32[]{:S(2)}) collective-permute-start(f32[32,512]{1,0:T(8,128)S(1)} %fusion), channel_id=1, source_target_pairs={{0,12},{4,16},{8,20},{12,24},{16,28},{20,32},{24,36},{28,40},{32,4... | collective-permute-start | bytes 196616
  1608.6 18.0 collective-permute-start.1
  1610.5 16.7 collective-permute-start
  1612.4 14.2 collective-permute-start.3
  1626.6 0.6 copy-start.4
Sparse Core Ops, SparseCore 0:
  17.0 695.0 all-reduce.8
  728.3 662.3 all-reduce.6
  1720.9 113.0 all-gather.2
where the time goes:
time: 1850 us; the launch traced here: 1840 us
  waiting for transfers between devices  1470 us (79%)
  blocking collectives  295 us (16%)
  matrix products  27.5 us (1%)
    psum x1, waiting for transfers between devices, local(): lax.psum((fresh_share * stats_a, fresh_share * stats_g), 'shard')  693 us
    psum x1, waiting for transfers between devices, local(): lax.psum((owner_part(slots_a, shard_pos, shard_count), owner_part(slots_g...  652 us
    unnamed x1, blocking collectives  198 us
    all_gather x1, waiting for transfers between devices, local(): lax.all_gather(weight_new.astype(jnp.bfloat16), 'shard', axis=0, tiled=True)  112 us
    psum x1, blocking collectives, local(): square_total = lax.psum(jnp.sum(precon * precon), ('shard', 'tensor'))  88.1 us
  transfers between devices with their start and end apart: 7, of which 4 were waited for; matrix products, arithmetic and copies ran while one was open for 1% of the time, Pallas kernels for 0%

commit v1 on v0

v1 whole, which is shorter than its diff:
```python
import functools

import jax
import jax.numpy as jnp
from jax import lax
from jax.experimental import pallas as pl
from jax.experimental.pallas import tpu as pltpu
from jax.sharding import PartitionSpec as P

NS_IT = 5
NX = 4
NT = 4
BLK = 128

factor_decay = 0.8
damping_rate = 0.03
momentum_rate = 0.9
decay_rate = 0.01
learn_rate = 0.05
epsilon_sq = 1e-06

MESH = pl.DeviceIdType.MESH
f32 = jnp.float32
bf16 = jnp.bfloat16


def split(a):
    hi = a.astype(bf16)
    return hi, (a - hi.astype(f32)).astype(bf16)


def dot(a, b):
    return lax.dot_general(a, b, (((1,), (0,)), ((), ())), preferred_element_type=f32)


def dot3(a, b):
    ah, al = split(a)
    bh, bl = split(b)
    return dot(ah, bh) + (dot(ah, bl) + dot(al, bh))


def newton_inverses(factors, widths):
    rows = lax.broadcasted_iota(jnp.int32, (BLK, BLK), 0)
    cols = lax.broadcasted_iota(jnp.int32, (BLK, BLK), 1)
    identity = (rows == cols).astype(f32)
    damped, guess = [], []
    for factor, width in zip(factors, widths):
        inside = ((rows == cols) & (rows < width)).astype(f32)
        trace_mean = jnp.sum(jnp.sum(factor * inside, axis=1, keepdims=True), axis=0, keepdims=True) / width
        m = factor + (damping_rate * trace_mean) * inside
        bound = jnp.max(jnp.sum(jnp.abs(m), axis=1, keepdims=True), axis=0, keepdims=True)
        damped.append(split(m))
        guess.append(inside / bound)
    for _ in range(NS_IT):
        halves = [split(x) for x in guess]
        product = [
            dot(mh, xh) + (dot(mh, xl) + dot(ml, xh)) for (mh, ml), (xh, xl) in zip(damped, halves)
        ]
        rest = [split(2.0 * identity - p) for p in product]
        guess = [
            dot(xh, rh) + (dot(xh, rl) + dot(xl, rh)) for (xh, xl), (rh, rl) in zip(halves, rest)
        ]
    return guess


def kernel(
    nq, samples, entries,
    own_a, own_g, inv_own_a, inv_own_g,
    picks_a, picks_g, raw, a_state, g_state, momentum, weight,
    a_new, g_new, mom_new, w_new, gathered,
    pa_in, pg_in, raw_in, gst_in, part, parta_in, partg_in, red, fac, inv_g, fac_a, fac_g,
    st, st_in, both, out_buf, out_in, sq, sq_in, sq2, sq2_in, wide,
    s_pa, r_pa, s_pg, r_pg, s_raw, r_raw, s_gst, r_gst, s_rsa, r_rsa, s_rsg, r_rsg,
    s_aga, r_aga, s_agg, r_agg, s_faca, r_faca, s_invg, r_invg, s_facg, r_facg,
    s_st, r_st, s_out, r_out, s_sq, r_sq, s_sq2, r_sq2, s_w1, r_w1, s_w2, r_w2,
):
    h = lax.axis_index("shard")
    t = lax.axis_index("tensor")
    q = h // NX
    x = lax.rem(h, NX)
    s = h // nq
    j = lax.rem(h, nq)
    bg = g_state.shape[-1]
    group = 5 * bg

    def send(src, dst, ssem, rsem, shard, tensor):
        pltpu.make_async_remote_copy(
            src_ref=src, dst_ref=dst, send_sem=ssem, recv_sem=rsem,
            device_id={"shard": shard, "tensor": tensor}, device_id_type=MESH,
        ).start()

    def wait(ref, sem):
        pltpu.make_async_copy(ref, ref, sem).wait()

    def each(me, fn):
        def body(k, c):
            fn(lax.rem(me + k, nq))
            return c
        lax.fori_loop(1, nq, body, 0)

    def each_q(fn):
        each(q, lambda q2: fn(q2, q2 * NX + x))

    def each_j(fn):
        each(j, lambda j2: fn(j2, s * nq + j2))

    def each_x(fn):
        for k in (1, 3, 2):
            x2 = lax.rem(x + k, NX)
            fn(x2, q * NX + x2)

    def each_s(fn):
        for k in (2, 1, 3):
            s2 = lax.rem(s + k, NT)
            fn(s2, s2 * nq + j)

    def each_t(fn):
        for k in range(1, NT):
            fn(lax.rem(t + k, NT))

    def plane(fn):
        def body(k, c):
            other = lax.rem(s * NT + t + k, NT * NT)
            fn(other // NT * nq + j, lax.rem(other, NT))
            return c
        lax.fori_loop(1, NT * NT, body, 0)

    barrier = pltpu.get_barrier_semaphore()

    def greet(shard, tensor):
        pl.semaphore_signal(
            barrier, inc=1, device_id={"shard": shard, "tensor": tensor}, device_id_type=MESH
        )

    plane(greet)
    each_q(lambda q2, h2: greet(h2, t))
    each_j(lambda j2, h2: greet(h2, t))
    pl.semaphore_wait(barrier, NT * NT - 1 + 2 * (nq - 1))

    each_x(lambda x2, h2: send(picks_a.at[x2], pa_in.at[x], s_pa, r_pa, h2, t))
    each_s(lambda s2, h2: send(picks_g.at[s2], pg_in.at[s], s_pg, r_pg, h2, t))

    @pl.when(t == s)
    def _():
        each_t(lambda t2: send(g_state, gst_in, s_gst, r_gst, h, t2))

    def cols_of(x2):
        return raw.at[:, pl.ds(pl.multiple_of(x2 * BLK, BLK), BLK)]

    each_x(lambda x2, h2: send(cols_of(x2), raw_in.at[x], s_raw, r_raw, h2, t))

    @pl.when(t == s)
    def _():
        gst_in[...] = g_state[...]

    def square_sum(v):
        return lax.dot_general(v, v, (((0,), (0,)), ((), ())), preferred_element_type=f32)

    pa_in[pl.ds(x, 1)] = picks_a[pl.ds(x, 1)]
    pg_in[pl.ds(s, 1)] = picks_g[pl.ds(s, 1)]
    wait(pa_in.at[pl.ds(0, NX - 1)], r_pa)
    part[2 * BLK : 3 * BLK] = square_sum(pa_in[...].reshape(-1, BLK))
    pa = BLK // nq
    pg = 2 * BLK // nq

    def rows_a(ref, k):
        return ref.at[pl.ds(pl.multiple_of(2 * BLK + k * pa, 8), pa)]

    def rows_g(ref, k):
        return ref.at[pl.ds(pl.multiple_of(k * pg, 8), pg)]

    each_q(lambda q2, h2: send(rows_a(part, q2), parta_in.at[q], s_rsa, r_rsa, h2, t))
    wait(pg_in.at[pl.ds(0, NT - 1)], r_pg)
    for k in range(2):
        part[k * BLK : (k + 1) * BLK] = square_sum(
            pg_in[:, :, k * BLK : (k + 1) * BLK].reshape(-1, BLK)
        )
    each_j(lambda j2, h2: send(rows_g(part, j2), partg_in.at[j], s_rsg, r_rsg, h2, t))
    parta_in[pl.ds(q, 1)] = rows_a(part, q)[...][None]
    partg_in[pl.ds(j, 1)] = rows_g(part, j)[...][None]
    wait(parta_in.at[pl.ds(0, nq - 1)], r_rsa)
    rows_a(red, q)[...] = jnp.sum(parta_in[...], axis=0)
    each_q(lambda q2, h2: send(rows_a(red, q), rows_a(red, q), s_aga, r_aga, h2, t))
    wait(partg_in.at[pl.ds(0, nq - 1)], r_rsg)
    rows_g(red, j)[...] = jnp.sum(partg_in[...], axis=0)
    each_j(lambda j2, h2: send(rows_g(red, j), rows_g(red, j), s_agg, r_agg, h2, t))

    @pl.when(t != s)
    def _():
        wait(gst_in, r_gst)

    fresh_share = (1.0 - factor_decay) / samples
    fac[...] = jnp.zeros_like(fac)
    fac[0, 0:bg, 0:bg] = factor_decay * gst_in[own_g[s, t]]
    fac[1, 0:bg, 0:bg] = factor_decay * gst_in[own_g[s, 4]]
    fac[2] = factor_decay * a_state[own_a[t, x]]
    wait(parta_in.at[pl.ds(0, nq - 1)], r_aga)
    wait(partg_in.at[pl.ds(0, nq - 1)], r_agg)
    for k in range(3):
        fac[k] = fac[k] + fresh_share * red[k * BLK : (k + 1) * BLK, :]

    inverses = newton_inverses([fac[0], fac[1], fac[2]], [bg, bg, BLK])
    inv_g[pl.ds(t, 1)] = inverses[0][None]
    inv_g[4] = inverses[1]
    inv_a = inverses[2]
    each_t(lambda t2: send(inv_g.at[t], inv_g.at[t], s_invg, r_invg, h, t2))

    raw_in[pl.ds(x, 1)] = cols_of(x)[...][None]
    wait(raw_in.at[pl.ds(0, NX - 1)], r_raw)
    for k in range(NT):
        r = slice(k * group, (k + 1) * group)
        st[k] = (raw_in[0, r] + raw_in[1, r]) + (raw_in[2, r] + raw_in[3, r])
    each_s(lambda s2, h2: send(st.at[s2], st_in.at[s], s_st, r_st, h2, t))
    st_in[pl.ds(s, 1)] = st[pl.ds(s, 1)]

    each_x(lambda x2, h2: send(fac.at[2], fac_a.at[x], s_faca, r_faca, h2, t))
    fac_a[pl.ds(x, 1)] = fac[2][None]

    @pl.when(t == s)
    def _():
        each_s(lambda s2, h2: send(fac.at[0], fac_g.at[t], s_facg, r_facg, h2, s))
        each_s(lambda s2, h2: send(fac.at[1], fac_g.at[4], s_facg, r_facg, h2, s))
        fac_g[pl.ds(t, 1)] = fac[0][None]
        fac_g[4] = fac[1]

    @pl.when(t != s)
    def _():
        for s2 in range(NT):
            send(fac.at[0], fac_g.at[t], s_facg, r_facg, s2 * nq + j, s)

    wait(inv_g.at[pl.ds(0, NT - 1)], r_invg)
    wait(st_in.at[pl.ds(0, NT - 1)], r_st)
    ah, al = split(inv_a)
    for b in range(5):
        r = slice(b * bg, (b + 1) * bg)
        total = (st_in[0, r] + st_in[1, r]) + (st_in[2, r] + st_in[3, r])
        lh, ll = split(dot3(inv_g[b, 0:bg, 0:bg], total))
        both[r] = dot(lh, ah) + (dot(lh, al) + dot(ll, ah))
    own_rows = momentum.shape[0]
    wide_rows = out_buf.shape[1]
    for k in range(nq):
        out_buf[k, 0:own_rows] = both[k * own_rows : (k + 1) * own_rows]
        out_buf[k, own_rows:wide_rows] = jnp.zeros((wide_rows - own_rows, BLK), f32)
    each_j(lambda j2, h2: send(out_buf.at[j2], out_in.at[j], s_out, r_out, h2, t))
    out_in[pl.ds(j, 1)] = out_buf[pl.ds(j, 1)]
    wait(out_in.at[pl.ds(0, nq - 1)], r_out)
    square = jnp.zeros((8, BLK), f32)
    for b in range(NX):
        precon = jnp.zeros((wide_rows, BLK), f32)
        for k in range(b, nq, NX):
            precon = precon + out_in[k]
        wide[:, b * BLK : (b + 1) * BLK] = precon
        square = square + jnp.sum((precon * precon).reshape(-1, 8, BLK), axis=0)
    sq[...] = square
    each_j(lambda j2, h2: send(sq, sq_in.at[j], s_sq, r_sq, h2, t))
    sq_in[pl.ds(j, 1)] = square[None]
    wait(sq_in.at[pl.ds(0, nq - 1)], r_sq)
    sq2[...] = jnp.sum(sq_in[...], axis=0)
    plane(lambda h2, t2: send(sq2, sq2_in.at[s * NT + t], s_sq2, r_sq2, h2, t2))
    sq2_in[pl.ds(s * NT + t, 1)] = sq2[...][None]
    wait(sq2_in.at[pl.ds(0, NT * NT - 1)], r_sq2)
    total = jnp.sum(sq2_in[...], axis=0)
    mean_sq = jnp.sum(jnp.sum(total, axis=1, keepdims=True), axis=0, keepdims=True) / entries
    update = wide[0:own_rows] / jnp.sqrt(mean_sq + epsilon_sq)
    momentum_new = momentum_rate * momentum[...] + update + decay_rate * weight[...]
    weight_new = weight[...] - learn_rate * momentum_new
    mom_new[...] = momentum_new
    w_new[...] = weight_new
    wide[0:own_rows] = weight_new
    gathered[pl.ds(x, 1), pl.ds(q, 1)] = wide[...].astype(bf16)[None, None]
    mine = gathered.at[x, q]
    each_q(lambda q2, h2: send(mine, mine, s_w1, r_w1, h2, t))

    wait(fac_a.at[pl.ds(0, NX - 1)], r_faca)

    @pl.when(t == s)
    def _():
        wait(fac_g.at[pl.ds(0, 3)], r_facg)

    @pl.when(t != s)
    def _():
        wait(fac_g, r_facg)

    for k in range(4):
        a_new[k] = fac_a[inv_own_a[t, k]]
    for k in range(5):
        g_new[k] = fac_g[inv_own_g[t, k], 0:bg, 0:bg]

    wait(gathered.at[0, pl.ds(0, nq - 1)], r_w1)
    each_x(lambda x2, h2: send(gathered.at[x], gathered.at[x], s_w2, r_w2, h2, t))
    wait(gathered.at[pl.ds(0, NX - 1)], r_w2)

    wait(pa_in.at[pl.ds(0, NX - 1)], s_pa)
    wait(pg_in.at[pl.ds(0, NT - 1)], s_pg)
    wait(raw_in.at[pl.ds(0, NX - 1)], s_raw)

    @pl.when(t == s)
    def _():
        for _ in range(NT - 1):
            wait(gst_in, s_gst)
        for _ in range(2):
            wait(fac_g.at[pl.ds(0, 3)], s_facg)

    @pl.when(t != s)
    def _():
        wait(fac_g.at[pl.ds(0, 4)], s_facg)

    for sem in (s_rsa, s_aga):
        wait(parta_in.at[pl.ds(0, nq - 1)], sem)
    for sem in (s_rsg, s_agg):
        wait(partg_in.at[pl.ds(0, nq - 1)], sem)
    wait(inv_g.at[pl.ds(0, NT - 1)], s_invg)
    wait(fac_a.at[pl.ds(0, NX - 1)], s_faca)
    wait(st_in.at[pl.ds(0, NT - 1)], s_st)
    wait(out_in.at[pl.ds(0, nq - 1)], s_out)
    wait(sq_in.at[pl.ds(0, nq - 1)], s_sq)
    wait(sq2_in.at[pl.ds(0, NT * NT - 1)], s_sq2)
    wait(gathered.at[0, pl.ds(0, nq - 1)], s_w1)
    wait(gathered.at[pl.ds(0, NX - 1)], s_w2)


def local(acts, out_grad, sample_rows, own_a, own_g, a_state, g_state, momentum, weight):
    shard_count = lax.axis_size("shard")
    tensor_count = lax.axis_size("tensor")
    t = lax.axis_index("tensor")
    nq = shard_count // NX
    tokens, cols = acts.shape
    picked_rows = sample_rows.shape[0]
    out_dim = out_grad.shape[1]
    own_rows = momentum.shape[0]
    wide_rows = (own_rows + 15) // 16 * 16
    bg = g_state.shape[-1]

    pick = (sample_rows[:, None] == jnp.arange(tokens, dtype=jnp.int32)[None, :]).astype(bf16)
    picked_a = jnp.dot(pick, acts, preferred_element_type=f32).astype(bf16)
    picked_g = jnp.dot(pick, out_grad, preferred_element_type=f32).astype(bf16)
    picks_a = picked_a.reshape(picked_rows, NX, BLK).transpose(1, 0, 2)
    blocks_g = picked_g.reshape(picked_rows, NT, 5, bg).transpose(1, 0, 2, 3)
    g_mine = lax.dynamic_index_in_dim(blocks_g, t, 2, keepdims=False)
    pad = ((0, 0), (0, 0), (0, BLK - bg))
    picks_g = jnp.concatenate([jnp.pad(g_mine, pad), jnp.pad(blocks_g[:, :, 4], pad)], axis=-1)
    raw = lax.dot_general(
        out_grad, acts, (((0,), (0,)), ((), ())), preferred_element_type=f32
    )
    slots_a = jnp.arange(own_a.shape[1], dtype=jnp.int32)
    slots_g = jnp.arange(own_g.shape[1], dtype=jnp.int32)
    inv_own_a = jnp.sum(jnp.where(own_a[:, None, :] == slots_a[None, :, None], slots_a, 0), axis=-1)
    inv_own_g = jnp.sum(jnp.where(own_g[:, None, :] == slots_g[None, :, None], slots_g, 0), axis=-1)

    smem = pl.BlockSpec(memory_space=pltpu.SMEM)
    vmem = pl.BlockSpec(memory_space=pltpu.VMEM)
    group = out_dim // NX
    dma = pltpu.SemaphoreType.DMA
    a_new, g_new, mom_new, w_new, gathered = pl.pallas_call(
        functools.partial(
            kernel, nq, picked_rows * shard_count, own_rows * shard_count * cols * tensor_count
        ),
        out_shape=(
            jax.ShapeDtypeStruct(a_state.shape[1:], f32),
            jax.ShapeDtypeStruct(g_state.shape[1:], f32),
            jax.ShapeDtypeStruct(momentum.shape, f32),
            jax.ShapeDtypeStruct(weight.shape, f32),
            jax.ShapeDtypeStruct((NX, nq, wide_rows, cols), bf16),
        ),
        in_specs=[smem] * 4 + [vmem] * 7,
        out_specs=(vmem,) * 5,
        scratch_shapes=[
            pltpu.VMEM(picks_a.shape, bf16),
            pltpu.VMEM(picks_g.shape, bf16),
            pltpu.VMEM((NX, out_dim, BLK), f32),
            pltpu.VMEM(g_state.shape[1:], f32),
            pltpu.VMEM((3 * BLK, BLK), f32),
            pltpu.VMEM((nq, BLK // nq, BLK), f32),
            pltpu.VMEM((nq, 2 * BLK // nq, BLK), f32),
            pltpu.VMEM((3 * BLK, BLK), f32),
            pltpu.VMEM((3, BLK, BLK), f32),
            pltpu.VMEM((5, BLK, BLK), f32),
            pltpu.VMEM((NX, BLK, BLK), f32),
            pltpu.VMEM((5, BLK, BLK), f32),
            pltpu.VMEM((NT, group, BLK), f32),
            pltpu.VMEM((NT, group, BLK), f32),
            pltpu.VMEM((group, BLK), f32),
            pltpu.VMEM((nq, wide_rows, BLK), f32),
            pltpu.VMEM((nq, wide_rows, BLK), f32),
            pltpu.VMEM((8, BLK), f32),
            pltpu.VMEM((nq, 8, BLK), f32),
            pltpu.VMEM((8, BLK), f32),
            pltpu.VMEM((NT * NT, 8, BLK), f32),
            pltpu.VMEM((wide_rows, cols), f32),
        ]
        + [dma] * 34,
        compiler_params=pltpu.CompilerParams(
            collective_id=0, has_side_effects=True, vmem_limit_bytes=48 * 1024 * 1024
        ),
    )(own_a, own_g, inv_own_a, inv_own_g, picks_a, picks_g, raw, a_state[0], g_state[0], momentum, weight)
    full = gathered[:, :, :own_rows].transpose(1, 0, 2, 3).reshape(out_dim, cols)
    return (a_new[None], g_new[None], mom_new, w_new, full)


def solution(mesh):
    return jax.shard_map(
        local,
        mesh=mesh,
        in_specs=(
            P("shard", "tensor"),
            P("shard", None),
            P("shard"),
            P(),
            P(),
            P("tensor", None, None, None),
            P("tensor", None, None, None),
            P("shard", "tensor"),
            P("shard", "tensor"),
        ),
        out_specs=(
            P("tensor", None, None, None),
            P("tensor", None, None, None),
            P("shard", "tensor"),
            P("shard", "tensor"),
            P(None, "tensor"),
        ),
        check_vma=False,
    )
```

time: 1850 us -> 180 us (0.10)
  waiting for transfers between devices: 1470 us -> 0 us
  blocking collectives: 295 us -> 0 us
  Pallas kernels: 0 us -> 153 us
    psum x2 -> x0, waiting for transfers between devices: 1340 us -> none  [the longest x1 693 us: local(): lax.psum((fresh_share * stats_a, fresh_share * stats_g), 'shard')]
    unnamed x1 -> x0, blocking collectives: 198 us -> none
    pallas_call x0 -> x1, Pallas kernels: none -> 153 us  [local(): pl.pallas_call(functools.partial(kernel, nq, picked_rows * shard_count, o...]
    all_gather x1 -> x0, waiting for transfers between devices: 112 us -> none  [local(): lax.all_gather(weight_new.astype(jnp.bfloat16), 'shard', axis=0, tiled=True)]
    psum x1 -> x0, blocking collectives: 88.1 us -> none  [local(): square_total = lax.psum(jnp.sum(precon * precon), ('shard', 'tensor'))]
  transfers between devices with their start and end apart: 7 -> 0, of which waited for: 4 -> 0; matrix products, arithmetic and copies ran while one was open for 1% -> 0% of each run, Pallas kernels for 0% -> 0%
where the time goes in v1:
time: 180 us
  Pallas kernels  153 us (85%)
  matrix products  15.4 us (9%)
  local copies, waits for them, and re-layouts  9.35 us (5%)
  other arithmetic  1.86 us (1%)
    pallas_call x1, Pallas kernels, local(): pl.pallas_call(functools.partial(kernel, nq, picked_rows * shard_count, o...  153 us
    dot_general x1, matrix products, local(): lax.dot_general(out_grad, acts, (((0,), (0,)), ((), ())), preferred_eleme...  9.43 us
    dot_general x1, matrix products, local(): picked_g = jnp.dot(pick, out_grad, preferred_element_type=f32).astype(bf16)  4.75 us
    reshape x1, local copies, waits for them, and re-layouts, local(): gathered[:, :, :own_rows].transpose(1, 0, 2, 3).reshape(out_dim, cols)  3.83 us

profile of v1, /device:TPU:24, one launch (start us, length us, event | category | flops | bytes accessed | tf_op | source)
XLA Modules:
  0.0 179.9 jit_solution(1446540164209540959)
XLA Ops:
  0.6 0.0 copy-start
  0.6 0.0 copy-start.7
  0.7 1.0 select_reduce_fusion.1.inv_own_a
  1.6 0.9 select_reduce_fusion
  2.5 0.1 copy.21.inv_own_g
  2.6 0.0 copy-done
  2.6 1.2 fusion
  3.8 0.0 copy-done.7
  3.8 4.7 %convolution_convert_fusion = bf16[64,1920]{1,0:T(8,128)(2,1)S(1)} fusion(bf16[2048,1920]{1,0:T(8,128)(2,1)} %param.10, s32[64]{0:T(128)S(1)} %copy-done.7), kind=kOutput, calls=%fused_computation | convolution fusion | flops 503570432 | bytes 8110336 | tf_op jit(solution)/shard_map/dot_general | solution.py:336
  8.6 0.6 reshape.23
  9.1 0.1 copy.27
  9.3 0.1 copy.19
  9.5 0.0 copy-start.1
  9.5 0.0 copy-start.2
  9.5 0.0 copy-start.3
  9.6 0.0 copy-start.4
  9.6 0.0 copy-start.5
  9.6 0.0 copy-start.6
  9.6 9.4 %fusion.6.raw = f32[1920,512]{1,0:T(8,128)} fusion(bf16[2048,1920]{1,0:T(8,128)(2,1)} %param.10, bf16[2048,512]{1,0:T(8,128)(2,1)S(1)} %copy-done), kind=kOutput, calls=%fused_computation.19 | convolution fusion | flops 4026531840 | bytes 13893632 | tf_op jit(solution)/shard_map/dot_general | solution.py:342
  19.0 0.0 copy-done.1
  19.0 0.0 copy-done.2
  19.0 0.0 copy-done.3
  19.0 0.0 copy-done.4
  19.0 0.0 copy-done.5
  19.0 0.0 copy-done.6
  19.1 152.6 %shard_map.128 = (f32[4,128,128]{2,1,0:T(8,128)S(1)}, f32[5,96,96]{2,1,0:T(8,128)S(1)}, f32[30,512]{1,0:T(8,128)S(1)}, f32[30,512]{1,0:T(8,128)S(1)}, bf16[4,16,32,512]{3,2,1,0:T(8,128)(2,1)S(1)}) custom-call(s32[4,4]{1,0:T(4,128)S(1)} %copy-done.6, s32[4,5]{1,0:T(4,128)S(1)} %copy-done.5, s32[4,4]{1,0:T(4,128)S(1)} %select_reduce_fusion.1.inv_own_a, ...), custom_call_target="tpu_custom_call" | custom-call | tf_op jit(solution)/shard_map/pallas_call | solution.py:354
  171.6 0.2 slice_bitcast_fusion
  171.9 1.6 copy.22
  173.5 3.8 %reshape.24 = bf16[1920,512]{1,0:T(8,128)(2,1)} reshape(bf16[16,4,30,512]{3,2,1,0:T(8,128)(2,1)} %copy.22) | data formatting | bytes 3932160 | tf_op jit(solution)/shard_map/reshape | solution.py:396
  177.3 0.7 copy.32
  178.0 0.7 copy.33
  178.7 0.6 copy.34
  179.3 0.6 copy.35
  (4 shorter events, 0.1 us)
Async XLA Ops:
  0.6 2.0 %copy-start = (bf16[2048,512]{1,0:T(8,128)(2,1)S(1)}, bf16[2048,512]{1,0:T(8,128)(2,1)}, u32[]{:S(2)}) copy-start(bf16[2048,512]{1,0:T(8,128)(2,1)} %param.9) | copy-start | bytes 6291460
  0.6 3.2 %copy-start.7 = (s32[64]{0:T(128)S(1)}, s32[64]{0:T(128)}, u32[]{:S(2)}) copy-start(s32[64]{0:T(128)} %param.11) | copy-start | bytes 772
  9.5 9.5 %copy-start.1 = (f32[1,4,128,128]{3,2,1,0:T(8,128)S(1)}, f32[1,4,128,128]{3,2,1,0:T(8,128)}, u32[]{:S(2)}) copy-start(f32[1,4,128,128]{3,2,1,0:T(8,128)} %param.14) | copy-start | bytes 786436
  9.5 9.5 %copy-start.2 = (f32[1,5,96,96]{3,2,1,0:T(8,128)S(1)}, f32[1,5,96,96]{3,2,1,0:T(8,128)}, u32[]{:S(2)}) copy-start(f32[1,5,96,96]{3,2,1,0:T(8,128)} %param.15) | copy-start | bytes 552964
  9.5 9.5 %copy-start.3 = (f32[30,512]{1,0:T(8,128)S(1)}, f32[30,512]{1,0:T(8,128)}, u32[]{:S(2)}) copy-start(f32[30,512]{1,0:T(8,128)} %momentum.1) | copy-start | bytes 184324
  9.6 9.5 %copy-start.4 = (f32[30,512]{1,0:T(8,128)S(1)}, f32[30,512]{1,0:T(8,128)}, u32[]{:S(2)}) copy-start(f32[30,512]{1,0:T(8,128)} %weight.1) | copy-start | bytes 184324
  9.6 9.5 %copy-start.5 = (s32[4,5]{1,0:T(4,128)S(1)}, s32[4,5]{1,0:T(4,128)}, u32[]{:S(2)}) copy-start(s32[4,5]{1,0:T(4,128)} %own_g.1) | copy-start | bytes 244
  9.6 9.5 %copy-start.6 = (s32[4,4]{1,0:T(4,128)S(1)}, s32[4,4]{1,0:T(4,128)}, u32[]{:S(2)}) copy-start(s32[4,4]{1,0:T(4,128)} %own_a.1) | copy-start | bytes 196

commit v2 on v1

--- a/solution.py
+++ b/solution.py
@@ -73,6 +73,7 @@
     s_pa, r_pa, s_pg, r_pg, s_raw, r_raw, s_gst, r_gst, s_rsa, r_rsa, s_rsg, r_rsg,
     s_aga, r_aga, s_agg, r_agg, s_faca, r_faca, s_invg, r_invg, s_facg, r_facg,
     s_st, r_st, s_out, r_out, s_sq, r_sq, s_sq2, r_sq2, s_w1, r_w1, s_w2, r_w2,
+    r_relay, r_half,
 ):
     h = lax.axis_index("shard")
     t = lax.axis_index("tensor")
@@ -147,7 +148,16 @@
     def cols_of(x2):
         return raw.at[:, pl.ds(pl.multiple_of(x2 * BLK, BLK), BLK)]
 
-    each_x(lambda x2, h2: send(cols_of(x2), raw_in.at[x], s_raw, r_raw, h2, t))
+    right, left, across = (lax.rem(x + k, NX) for k in (1, 3, 2))
+    h_right, h_left = q * NX + right, q * NX + left
+    half = raw.shape[0] // 2
+    top, bottom = pl.ds(0, half), pl.ds(half, half)
+
+    def half_of(rows, x2):
+        return raw.at[rows, pl.ds(pl.multiple_of(x2 * BLK, BLK), BLK)]
+
+    send(half_of(top, across), raw_in.at[2, top], s_raw, r_relay, h_right, t)
+    send(half_of(bottom, across), raw_in.at[2, bottom], s_raw, r_relay, h_left, t)
 
     @pl.when(t == s)
     def _():
@@ -176,6 +186,8 @@
             pg_in[:, :, k * BLK : (k + 1) * BLK].reshape(-1, BLK)
         )
     each_j(lambda j2, h2: send(rows_g(part, j2), partg_in.at[j], s_rsg, r_rsg, h2, t))
+    send(half_of(bottom, right), raw_in.at[0, bottom], s_raw, r_raw, h_right, t)
+    send(half_of(top, left), raw_in.at[1, top], s_raw, r_raw, h_left, t)
     parta_in[pl.ds(q, 1)] = rows_a(part, q)[...][None]
     partg_in[pl.ds(j, 1)] = rows_g(part, j)[...][None]
     wait(parta_in.at[pl.ds(0, nq - 1)], r_rsa)
@@ -184,6 +196,12 @@
     wait(partg_in.at[pl.ds(0, nq - 1)], r_rsg)
     rows_g(red, j)[...] = jnp.sum(partg_in[...], axis=0)
     each_j(lambda j2, h2: send(rows_g(red, j), rows_g(red, j), s_agg, r_agg, h2, t))
+
+    wait(raw_in.at[2], r_relay)
+    raw_in[3, top] = raw_in[2, top] + half_of(top, right)[...]
+    raw_in[3, bottom] = raw_in[2, bottom] + half_of(bottom, left)[...]
+    send(raw_in.at[3, top], raw_in.at[0, top], s_raw, r_raw, h_right, t)
+    send(raw_in.at[3, bottom], raw_in.at[1, bottom], s_raw, r_raw, h_left, t)
 
     @pl.when(t != s)
     def _():
@@ -205,11 +223,11 @@
     inv_a = inverses[2]
     each_t(lambda t2: send(inv_g.at[t], inv_g.at[t], s_invg, r_invg, h, t2))
 
-    raw_in[pl.ds(x, 1)] = cols_of(x)[...][None]
-    wait(raw_in.at[pl.ds(0, NX - 1)], r_raw)
+    wait(raw_in.at[pl.ds(0, 2)], r_raw)
+    mine_raw = cols_of(x)
     for k in range(NT):
         r = slice(k * group, (k + 1) * group)
-        st[k] = (raw_in[0, r] + raw_in[1, r]) + (raw_in[2, r] + raw_in[3, r])
+        st[k] = (raw_in[0, r] + raw_in[1, r]) + mine_raw[r]
     each_s(lambda s2, h2: send(st.at[s2], st_in.at[s], s_st, r_st, h2, t))
     st_in[pl.ds(s, 1)] = st[pl.ds(s, 1)]
 
@@ -287,8 +305,19 @@
         g_new[k] = fac_g[inv_own_g[t, k], 0:bg, 0:bg]
 
     wait(gathered.at[0, pl.ds(0, nq - 1)], r_w1)
-    each_x(lambda x2, h2: send(gathered.at[x], gathered.at[x], s_w2, r_w2, h2, t))
-    wait(gathered.at[pl.ds(0, NX - 1)], r_w2)
+    first, second = pl.ds(0, nq // 2), pl.ds(nq // 2, nq // 2)
+
+    def spread(x2, part_q, rsem, shard):
+        send(gathered.at[x2, part_q], gathered.at[x2, part_q], s_w2, rsem, shard, t)
+
+    spread(x, first, r_half, h_right)
+    spread(x, second, r_half, h_left)
+    spread(x, second, r_w2, h_right)
+    spread(x, first, r_w2, h_left)
+    wait(gathered.at[0], r_half)
+    spread(left, first, r_w2, h_right)
+    spread(right, second, r_w2, h_left)
+    wait(gathered.at[pl.ds(0, 2)], r_w2)
 
     wait(pa_in.at[pl.ds(0, NX - 1)], s_pa)
     wait(pg_in.at[pl.ds(0, NT - 1)], s_pg)
@@ -388,7 +417,7 @@
             pltpu.VMEM((NT * NT, 8, BLK), f32),
             pltpu.VMEM((wide_rows, cols), f32),
         ]
-        + [dma] * 34,
+        + [dma] * 36,
         compiler_params=pltpu.CompilerParams(
             collective_id=0, has_side_effects=True, vmem_limit_bytes=48 * 1024 * 1024
         ),

time: 180 us -> 158 us (0.88)
  Pallas kernels: 153 us -> 130 us
    pallas_call x1, Pallas kernels: 153 us -> 130 us  [local(): pl.pallas_call(functools.partial(kernel, nq, picked_rows * shard_count, o...]
where the time goes in v2:
time: 158 us; the launch traced here: 157 us
  Pallas kernels  130 us (82%)
  matrix products  15.4 us (10%)
  local copies, waits for them, and re-layouts  9.35 us (6%)
  other arithmetic  1.86 us (1%)
    pallas_call x1, Pallas kernels, local(): pl.pallas_call(functools.partial(kernel, nq, picked_rows * shard_count, o...  130 us
    dot_general x1, matrix products, local(): lax.dot_general(out_grad, acts, (((0,), (0,)), ((), ())), preferred_eleme...  9.43 us
    dot_general x1, matrix products, local(): picked_g = jnp.dot(pick, out_grad, preferred_element_type=f32).astype(bf16)  4.75 us
    reshape x1, local copies, waits for them, and re-layouts, local(): gathered[:, :, :own_rows].transpose(1, 0, 2, 3).reshape(out_dim, cols)  3.83 us

profile of v2, /device:TPU:24, one launch (start us, length us, event | category | flops | bytes accessed | tf_op | source)
XLA Modules:
  0.0 157.3 jit_solution(17022923082472678524)
XLA Ops:
  0.6 0.0 copy-start
  0.6 0.0 copy-start.7
  0.7 1.0 select_reduce_fusion.1.inv_own_a
  1.6 0.9 select_reduce_fusion
  2.5 0.1 copy.21.inv_own_g
  2.6 0.0 copy-done
  2.6 1.2 fusion
  3.8 0.0 copy-done.7
  3.8 4.7 %convolution_convert_fusion = bf16[64,1920]{1,0:T(8,128)(2,1)S(1)} fusion(bf16[2048,1920]{1,0:T(8,128)(2,1)} %param.10, s32[64]{0:T(128)S(1)} %copy-done.7), kind=kOutput, calls=%fused_computation | convolution fusion | flops 503570432 | bytes 8110336 | tf_op jit(solution)/shard_map/dot_general | solution.py:365
  8.6 0.6 reshape.23
  9.1 0.1 copy.27
  9.3 0.1 copy.19
  9.5 0.0 copy-start.1
  9.5 0.0 copy-start.2
  9.5 0.0 copy-start.3
  9.6 0.0 copy-start.4
  9.6 0.0 copy-start.5
  9.6 0.0 copy-start.6
  9.6 9.4 %fusion.6.raw = f32[1920,512]{1,0:T(8,128)} fusion(bf16[2048,1920]{1,0:T(8,128)(2,1)} %param.10, bf16[2048,512]{1,0:T(8,128)(2,1)S(1)} %copy-done), kind=kOutput, calls=%fused_computation.19 | convolution fusion | flops 4026531840 | bytes 13893632 | tf_op jit(solution)/shard_map/dot_general | solution.py:371
  19.0 0.0 copy-done.1
  19.0 0.0 copy-done.2
  19.0 0.0 copy-done.3
  19.0 0.0 copy-done.4
  19.0 0.0 copy-done.5
  19.0 0.0 copy-done.6
  19.1 129.9 %shard_map.128 = (f32[4,128,128]{2,1,0:T(8,128)S(1)}, f32[5,96,96]{2,1,0:T(8,128)S(1)}, f32[30,512]{1,0:T(8,128)S(1)}, f32[30,512]{1,0:T(8,128)S(1)}, bf16[4,16,32,512]{3,2,1,0:T(8,128)(2,1)S(1)}) custom-call(s32[4,4]{1,0:T(4,128)S(1)} %copy-done.6, s32[4,5]{1,0:T(4,128)S(1)} %copy-done.5, s32[4,4]{1,0:T(4,128)S(1)} %select_reduce_fusion.1.inv_own_a, ...), custom_call_target="tpu_custom_call" | custom-call | tf_op jit(solution)/shard_map/pallas_call | solution.py:383
  149.0 0.2 slice_bitcast_fusion
  149.2 1.6 %copy.22 = bf16[16,4,30,512]{3,2,1,0:T(8,128)(2,1)} copy(bf16[16,4,30,512]{3,2,0,1:T(8,128)(2,1)S(1)} %slice_bitcast_fusion) | data formatting | bytes 3932160 | tf_op jit(solution)/shard_map/transpose | solution.py:425
  150.8 3.8 %reshape.24 = bf16[1920,512]{1,0:T(8,128)(2,1)} reshape(bf16[16,4,30,512]{3,2,1,0:T(8,128)(2,1)} %copy.22) | data formatting | bytes 3932160 | tf_op jit(solution)/shard_map/reshape | solution.py:425
  154.6 0.7 copy.32
  155.3 0.7 copy.33
  156.0 0.6 copy.34
  156.6 0.6 copy.35
  (4 shorter events, 0.1 us)
Async XLA Ops:
  0.6 2.0 %copy-start = (bf16[2048,512]{1,0:T(8,128)(2,1)S(1)}, bf16[2048,512]{1,0:T(8,128)(2,1)}, u32[]{:S(2)}) copy-start(bf16[2048,512]{1,0:T(8,128)(2,1)} %param.9) | copy-start | bytes 6291460
  0.6 3.2 %copy-start.7 = (s32[64]{0:T(128)S(1)}, s32[64]{0:T(128)}, u32[]{:S(2)}) copy-start(s32[64]{0:T(128)} %param.11) | copy-start | bytes 772
  9.5 9.5 %copy-start.1 = (f32[1,4,128,128]{3,2,1,0:T(8,128)S(1)}, f32[1,4,128,128]{3,2,1,0:T(8,128)}, u32[]{:S(2)}) copy-start(f32[1,4,128,128]{3,2,1,0:T(8,128)} %param.14) | copy-start | bytes 786436
  9.5 9.5 %copy-start.2 = (f32[1,5,96,96]{3,2,1,0:T(8,128)S(1)}, f32[1,5,96,96]{3,2,1,0:T(8,128)}, u32[]{:S(2)}) copy-start(f32[1,5,96,96]{3,2,1,0:T(8,128)} %param.15) | copy-start | bytes 552964
  9.5 9.5 %copy-start.3 = (f32[30,512]{1,0:T(8,128)S(1)}, f32[30,512]{1,0:T(8,128)}, u32[]{:S(2)}) copy-start(f32[30,512]{1,0:T(8,128)} %momentum.1) | copy-start | bytes 184324
  9.6 9.5 %copy-start.4 = (f32[30,512]{1,0:T(8,128)S(1)}, f32[30,512]{1,0:T(8,128)}, u32[]{:S(2)}) copy-start(f32[30,512]{1,0:T(8,128)} %weight.1) | copy-start | bytes 184324
  9.6 9.5 %copy-start.5 = (s32[4,5]{1,0:T(4,128)S(1)}, s32[4,5]{1,0:T(4,128)}, u32[]{:S(2)}) copy-start(s32[4,5]{1,0:T(4,128)} %own_g.1) | copy-start | bytes 244
  9.6 9.5 %copy-start.6 = (s32[4,4]{1,0:T(4,128)S(1)}, s32[4,4]{1,0:T(4,128)}, u32[]{:S(2)}) copy-start(s32[4,4]{1,0:T(4,128)} %own_a.1) | copy-start | bytes 196
